TPU v7x, 32 devices: a whole 2x2x4 slice. The times are simulated.
32 devices in a mesh: row: 4 (over z), col: 8 (over y, x, core).
Axes of the slice: x: 2, y: 2, z: 4, core: 2. Of those that a mesh axis runs over, the one named last changes fastest.
Arguments:
- embedding: float32 [4096, 256], P(('row', 'col')), may hold values from -6 to 6
- seed_cluster: int32 [4096], P(('row', 'col')), may hold values from 0 to 127
Outputs:
- log_member: float32 [4096, 128], P(('row', 'col'))
All inputs are finite; a program needn't handle non-finite values.
Results may differ from a plain program's by a relative error of at most 0.0003.
Values sent between devices are 32-bit elements; how exact they have to be, the bound alone decides.
A program may use at most 64 MiB of HBM per device.

v0:
```python
import jax
import jax.numpy as jnp
from jax import lax
from jax.sharding import PartitionSpec as P

CLUSTER_COUNT = 128
SWEEPS = 2
ANNEAL_TEMP_VALUE = 0.02


def shards(embedding, seed_cluster):
    per_device = embedding.shape[0]
    row_coords = lax.all_gather(embedding, "col", axis=0, tiled=True)
    col_coords, col_seeds = (
        lax.all_gather(embedding, "row", axis=0, tiled=True),
        lax.all_gather(seed_cluster, "row", axis=0, tiled=True),
    )
    row_sq = jnp.sum(row_coords * row_coords, axis=1)
    col_sq = jnp.sum(col_coords * col_coords, axis=1)
    inner = jnp.dot(row_coords, col_coords.T, precision=lax.Precision.HIGHEST)
    distance = jnp.sqrt(row_sq[:, None] + col_sq[None, :] - 2.0 * inner + 1.0)
    cluster_labels = jnp.arange(CLUSTER_COUNT, dtype=jnp.int32)
    member_cols = (
        0.5 * (col_seeds[:, None] == cluster_labels[None, :]).astype(jnp.float32)
        + 0.5 / CLUSTER_COUNT
    )
    member_own = (
        0.5 * (seed_cluster[:, None] == cluster_labels[None, :]).astype(jnp.float32)
        + 0.5 / CLUSTER_COUNT
    )
    log_member = jnp.zeros((per_device, CLUSTER_COUNT), jnp.float32)
    for sweep in range(SWEEPS):
        columns = member_cols
        attraction = lax.psum_scatter(
            jnp.dot(distance, columns, precision=lax.Precision.HIGHEST),
            "col",
            scatter_dimension=0,
            tiled=True,
        )
        counts, cohesion = lax.psum(
            (jnp.sum(member_own, axis=0), jnp.sum(member_own * attraction, axis=0)), ("row", "col")
        )
        pair_energy = attraction / counts[None, :] - cohesion[None, :] / (
            2.0 * counts[None, :] ** 2
        )
        member_logits = -pair_energy / ANNEAL_TEMP_VALUE
        highest = jnp.max(member_logits, axis=1, keepdims=True)
        log_member = (
            member_logits
            - highest
            - jnp.log(jnp.sum(jnp.exp(member_logits - highest), axis=1, keepdims=True))
        )
        member_own = jnp.exp(log_member)
        if sweep + 1 < SWEEPS:
            member_cols = lax.all_gather(member_own, "row", axis=0, tiled=True)
    return log_member


def solution(mesh):
    return jax.shard_map(
        shards,
        mesh=mesh,
        in_specs=(P(("row", "col"), None), P(("row", "col"))),
        out_specs=P(("row", "col"), None),
        check_vma=False,
    )
```

profile of v0, /device:TPU:0, one launch (start us, length us, event | category | flops | bytes accessed | tf_op | source)
XLA Modules:
  0.0 222.9 jit_solution(15321643899458992196)
XLA Ops:
  6.5 0.0 all-gather.3.cloned.1.call-start
  6.5 0.7 all-gather.3.cloned.1.call-update
  7.3 0.0 reduce-scatter.3.cloned.1.call-start
  7.3 12.8 %all-gather = s32[4,1,128]{2,1,0:T(1,128)S(1)} all-gather(s32[1,1,128]{2,1,0:T(1,128)} %bitcast.8), channel_id=1, replica_groups=mesh['row'=4,'col'=8] {'row'}, dimensions={0}, use_global_device_ids=true | all-gather | bytes 2560 | tf_op jit(solution)/shard_map/all_gather | solution.py:16
  20.1 15.0 %all_gather.13 = f32[512,256]{1,0:T(8,128)S(1)} all-gather(f32[128,256]{1,0:T(8,128)} %param.2), channel_id=1, replica_groups=mesh['row'=4,'col'=8] {'row'}, dimensions={0}, use_global_device_ids=true | all-gather | bytes 655360 | tf_op jit(solution)/shard_map/all_gather | solution.py:15
  35.1 0.1 multiply_reduce_fusion.1
  35.2 0.1 all-gather.3.cloned.1.call-done
  35.3 1.4 multiply_reduce_fusion
  36.8 3.9 %add_sqrt_fusion = f32[1024,512]{1,0:T(8,128)S(1)} fusion(f32[1024,256]{1,0:T(8,128)} %all-gather.3.cloned.1.call-done, f32[512,256]{1,0:T(8,128)S(1)} %all_gather.13, f32[512]{0:T(512)S(1)} %multiply_reduce_fusion.1, f32[1024]{0:T(1024)S(1)} %multiply_reduce_fusion), kind=kOutput, calls=%fused_computation | convolution fusion | flops 1612709888 | bytes 3676160 | tf_op jit(solution)/shard_map/dot_general | solution.py:20
  40.7 0.0 copy-start.1
  40.7 2.7 %fusion = f32[1024,128]{1,0:T(8,128)} fusion(f32[1024,512]{1,0:T(8,128)S(1)} %add_sqrt_fusion, s32[512]{0:T(512)S(1)} %bitcast.7), kind=kOutput, calls=%fused_computation.3 | convolution fusion | flops 805502976 | bytes 2623488 | tf_op jit(solution)/shard_map/dot_general | solution.py:35
  43.3 0.0 reduce-scatter.3.cloned.1.call-update
  43.4 0.0 reduce-scatter.5.cloned.1.call-start
  43.4 34.2 %reduce-scatter.3.cloned.1.call-done = f32[128,128]{1,0:T(8,128)} async-done(((f32[1024,128]{1,0:T(8,128)}), f32[128,128]{1,0:T(8,128)}) %reduce-scatter.3.cloned.1.call-update) | async-done | bytes 65552 | tf_op jit(solution)/shard_map/reduce_scatter | solution.py:34
  77.6 0.0 copy-done.1
  77.6 0.0 copy-start
  77.6 1.0 fusion.7
  78.7 39.3 %all-reduce.1 = (f32[128]{0:T(128)S(1)}, f32[128]{0:T(128)S(1)}) all-reduce(f32[128]{0:T(128)S(1)} %get-tuple-element.8, f32[128]{0:T(128)S(1)} %get-tuple-element.7), channel_id=1, replica_groups=mesh['row'=4,'col'=8] {'row','col'}, use_global_device_ids=true, to_apply=%region_6.0 | all-reduce | flops 256 | bytes 2048 | tf_op jit(solution)/shard_map/psum | solution.py:40
  118.0 1.0 fusion.11
  118.9 1.0 exponential_reduce_fusion.1
  120.0 1.0 subtract_exponential_fusion
  120.9 14.4 %all_gather.15 = f32[512,128]{1,0:T(8,128)S(1)} all-gather(f32[128,128]{1,0:T(8,128)S(1)} %subtract_exponential_fusion), channel_id=1, replica_groups=mesh['row'=4,'col'=8] {'row'}, dimensions={0}, use_global_device_ids=true | all-gather | bytes 327680 | tf_op jit(solution)/shard_map/all_gather | solution.py:55
  135.3 2.6 %fusion.14 = f32[1024,128]{1,0:T(8,128)} fusion(f32[1024,512]{1,0:T(8,128)S(1)} %add_sqrt_fusion, f32[512,128]{1,0:T(8,128)S(1)} %all_gather.15), kind=kOutput, calls=%fused_computation.30 | convolution fusion | flops 805306368 | bytes 2883584 | tf_op jit(solution)/shard_map/dot_general | solution.py:35
  137.9 0.0 reduce-scatter.5.cloned.1.call-update
  137.9 34.6 %reduce-scatter.5.cloned.1.call-done = f32[128,128]{1,0:T(8,128)} async-done(((f32[1024,128]{1,0:T(8,128)}), f32[128,128]{1,0:T(8,128)}) %reduce-scatter.5.cloned.1.call-update) | async-done | bytes 65552 | tf_op jit(solution)/shard_map/reduce_scatter | solution.py:34
  172.5 0.0 copy-done
  172.5 1.0 fusion.13
  173.5 39.3 %all-reduce = (f32[128]{0:T(128)S(1)}, f32[128]{0:T(128)S(1)}) all-reduce(f32[128]{0:T(128)S(1)} %get-tuple-element.6, f32[128]{0:T(128)S(1)} %get-tuple-element.5), channel_id=1, replica_groups=mesh['row'=4,'col'=8] {'row','col'}, use_global_device_ids=true, to_apply=%region_13.0 | all-reduce | flops 256 | bytes 2048 | tf_op jit(solution)/shard_map/psum | solution.py:40
  212.8 1.0 fusion.12
  213.7 1.0 exponential_reduce_fusion
  214.8 1.6 subtract_subtract_fusion
  (4 shorter events, 0.0 us)
Async XLA Ops:
  6.5 28.8 %all-gather.3.cloned.1.call-start = ((), (), s32[]{:S(2)}) async-start(), calls=%async_computation.2 | async-start | bytes 1179648 | tf_op jit(solution)/shard_map/all_gather | solution.py:13
  7.3 70.4 %reduce-scatter.3.cloned.1.call-start = ((), (), s32[]{:S(2)}) async-start(), calls=%async_computation.3 | async-start | bytes 589824 | tf_op jit(solution)/shard_map/reduce_scatter | solution.py:34
  40.7 37.0 %copy-start.1 = (s32[128]{0:T(128)S(1)}, s32[128]{0:T(128)}, u32[]{:S(2)}) copy-start(s32[128]{0:T(128)} %param.3) | copy-start | bytes 1540
  43.4 129.1 %reduce-scatter.5.cloned.1.call-start = ((), (), s32[]{:S(2)}) async-start(), calls=%async_computation.4 | async-start | bytes 589824 | tf_op jit(solution)/shard_map/reduce_scatter | solution.py:34
  77.6 94.8 %copy-start = (f32[128,128]{1,0:T(8,128)S(1)}, f32[128,128]{1,0:T(8,128)}, u32[]{:S(2)}) copy-start(f32[128,128]{1,0:T(8,128)} %reduce-scatter.3.cloned.1.call-done) | copy-start | bytes 196612
Sparse Core Ops, SparseCore 0:
  9.2 26.0 all-gather.2
  43.5 34.1 reduce-scatter.2
  138.0 34.4 reduce-scatter.4
where the time goes:
time: 224 us; the launch traced here: 223 us
  blocking collectives  121 us (54%)
  waiting for transfers between devices  69.7 us (31%)
  between operations  13.2 us (6%)
  other arithmetic  10 us (4%)
  matrix products  9.11 us (4%)
    psum x2, blocking collectives, shards(): lax.psum((jnp.sum(member_own, axis=0), jnp.sum(member_own * attraction, a...  78.6 us
    reduce_scatter x2, waiting for transfers between devices, shards(): lax.psum_scatter(jnp.dot(distance, columns, precision=lax.Precision.HIGHE...  68.8 us
    all_gather x1, blocking collectives, shards(): lax.all_gather(embedding, 'row', axis=0, tiled=True)  15 us
    all_gather x1, blocking collectives, shards(): member_cols = lax.all_gather(member_own, 'row', axis=0, tiled=True)  14.4 us
    all_gather x1, blocking collectives, shards(): lax.all_gather(seed_cluster, 'row', axis=0, tiled=True)  12.8 us
    dot_general x2, matrix products, shards(): jnp.dot(distance, columns, precision=lax.Precision.HIGHEST)  5.25 us
  transfers between devices with their start and end apart: 3, of which 3 were waited for; matrix products, arithmetic and copies ran while one was open for 0% of the time, Pallas kernels for 0%

commit v1 on v0

--- a/solution.py
+++ b/solution.py
@@ -38,7 +38,10 @@
             tiled=True,
         )
         counts, cohesion = lax.psum(
-            (jnp.sum(member_own, axis=0), jnp.sum(member_own * attraction, axis=0)), ("row", "col")
+            lax.psum(
+                (jnp.sum(member_own, axis=0), jnp.sum(member_own * attraction, axis=0)), "col"
+            ),
+            "row",
         )
         pair_energy = attraction / counts[None, :] - cohesion[None, :] / (
             2.0 * counts[None, :] ** 2

time: 224 us -> 189 us (0.84)
  blocking collectives: 121 us -> 89.2 us
  waiting for transfers between devices: 69.7 us -> 67 us
    psum x2, blocking collectives: 78.6 us -> 24.3 us  [shards(): lax.psum((jnp.sum(member_own, axis=0), jnp.sum(member_own * attraction, a...]
    psum x0 -> x2, blocking collectives: none -> 23.3 us  [shards(): lax.psum(lax.psum((jnp.sum(member_own, axis=0), jnp.sum(member_own * attr...]
    reduce_scatter x2, waiting for transfers between devices: 68.8 us -> 66.1 us  [shards(): lax.psum_scatter(jnp.dot(distance, columns, precision=lax.Precision.HIGHE...]
where the time goes in v1:
time: 189 us
  blocking collectives  89.2 us (47%)
  waiting for transfers between devices  67 us (35%)
  between operations  13.2 us (7%)
  other arithmetic  10.1 us (5%)
  matrix products  9.11 us (5%)
    reduce_scatter x2, waiting for transfers between devices, shards(): lax.psum_scatter(jnp.dot(distance, columns, precision=lax.Precision.HIGHE...  66.1 us
    psum x2, blocking collectives, shards(): lax.psum((jnp.sum(member_own, axis=0), jnp.sum(member_own * attraction, a...  24.3 us
    psum x2, blocking collectives, shards(): lax.psum(lax.psum((jnp.sum(member_own, axis=0), jnp.sum(member_own * attr...  23.3 us
    all_gather x1, blocking collectives, shards(): lax.all_gather(embedding, 'row', axis=0, tiled=True)  15 us
    all_gather x1, blocking collectives, shards(): member_cols = lax.all_gather(member_own, 'row', axis=0, tiled=True)  13.8 us
    all_gather x1, blocking collectives, shards(): lax.all_gather(seed_cluster, 'row', axis=0, tiled=True)  12.8 us
    dot_general x2, matrix products, shards(): jnp.dot(distance, columns, precision=lax.Precision.HIGHEST)  5.25 us
    dot_general x1, matrix products, shards(): inner = jnp.dot(row_coords, col_coords.T, precision=lax.Precision.HIGHEST)  3.86 us
  transfers between devices with their start and end apart: 3, of which 3 were waited for; matrix products, arithmetic and copies ran while one was open for 0% of the time, Pallas kernels for 0%

profile of v1, /device:TPU:0, one launch (start us, length us, event | category | flops | bytes accessed | tf_op | source)
XLA Modules:
  0.0 188.6 jit_solution(1975111163236927728)
XLA Ops:
  6.5 0.0 all-gather.3.cloned.1.call-start
  6.5 0.7 all-gather.3.cloned.1.call-update
  7.3 0.0 reduce-scatter.3.cloned.1.call-start
  7.3 12.8 %all-gather = s32[4,1,128]{2,1,0:T(1,128)S(1)} all-gather(s32[1,1,128]{2,1,0:T(1,128)} %bitcast.8), channel_id=1, replica_groups=mesh['row'=4,'col'=8] {'row'}, dimensions={0}, use_global_device_ids=true | all-gather | bytes 2560 | tf_op jit(solution)/shard_map/all_gather | solution.py:16
  20.1 15.0 %all_gather.13 = f32[512,256]{1,0:T(8,128)S(1)} all-gather(f32[128,256]{1,0:T(8,128)} %param.2), channel_id=1, replica_groups=mesh['row'=4,'col'=8] {'row'}, dimensions={0}, use_global_device_ids=true | all-gather | bytes 655360 | tf_op jit(solution)/shard_map/all_gather | solution.py:15
  35.1 0.1 multiply_reduce_fusion.1
  35.2 0.1 all-gather.3.cloned.1.call-done
  35.3 1.4 multiply_reduce_fusion
  36.8 3.9 %add_sqrt_fusion = f32[1024,512]{1,0:T(8,128)S(1)} fusion(f32[1024,256]{1,0:T(8,128)} %all-gather.3.cloned.1.call-done, f32[512,256]{1,0:T(8,128)S(1)} %all_gather.13, f32[512]{0:T(512)S(1)} %multiply_reduce_fusion.1, f32[1024]{0:T(1024)S(1)} %multiply_reduce_fusion), kind=kOutput, calls=%fused_computation | convolution fusion | flops 1612709888 | bytes 3676160 | tf_op jit(solution)/shard_map/dot_general | solution.py:20
  40.7 0.0 copy-start.1
  40.7 2.7 %fusion = f32[1024,128]{1,0:T(8,128)} fusion(f32[1024,512]{1,0:T(8,128)S(1)} %add_sqrt_fusion, s32[512]{0:T(512)S(1)} %bitcast.7), kind=kOutput, calls=%fused_computation.3 | convolution fusion | flops 805502976 | bytes 2623488 | tf_op jit(solution)/shard_map/dot_general | solution.py:35
  43.3 0.0 reduce-scatter.3.cloned.1.call-update
  43.4 0.0 reduce-scatter.5.cloned.1.call-start
  43.4 34.2 %reduce-scatter.3.cloned.1.call-done = f32[128,128]{1,0:T(8,128)} async-done(((f32[1024,128]{1,0:T(8,128)}), f32[128,128]{1,0:T(8,128)}) %reduce-scatter.3.cloned.1.call-update) | async-done | bytes 65552 | tf_op jit(solution)/shard_map/reduce_scatter | solution.py:34
  77.6 0.0 copy-done.1
  77.6 1.0 fusion.7
  78.7 12.2 %all-reduce.1 = (f32[128]{0:T(128)S(1)}, f32[128]{0:T(128)S(1)}) all-reduce(f32[128]{0:T(128)S(1)} %get-tuple-element.8, f32[128]{0:T(128)S(1)} %get-tuple-element.7), channel_id=1, replica_groups=mesh['row'=4,'col'=8] {'col'}, use_global_device_ids=true, to_apply=%region_7.0 | all-reduce | flops 256 | bytes 2048 | tf_op jit(solution)/shard_map/psum | solution.py:41
  90.8 11.7 %all-reduce.3 = (f32[128]{0:T(128)S(1)}, f32[128]{0:T(128)S(1)}) all-reduce(f32[128]{0:T(128)S(1)} %get-tuple-element.11, f32[128]{0:T(128)S(1)} %get-tuple-element.12), channel_id=1, replica_groups=mesh['row'=4,'col'=8] {'row'}, use_global_device_ids=true, to_apply=%region_8.0 | all-reduce | flops 256 | bytes 2048 | tf_op jit(solution)/shard_map/psum | solution.py:40
  102.5 1.0 fusion.11
  103.4 1.0 exponential_reduce_fusion.1
  104.5 1.0 subtract_exponential_fusion
  105.4 13.8 %all_gather.15 = f32[512,128]{1,0:T(8,128)S(1)} all-gather(f32[128,128]{1,0:T(8,128)S(1)} %subtract_exponential_fusion), channel_id=1, replica_groups=mesh['row'=4,'col'=8] {'row'}, dimensions={0}, use_global_device_ids=true | all-gather | bytes 327680 | tf_op jit(solution)/shard_map/all_gather | solution.py:58
  119.2 2.6 %fusion.14 = f32[1024,128]{1,0:T(8,128)} fusion(f32[1024,512]{1,0:T(8,128)S(1)} %add_sqrt_fusion, f32[512,128]{1,0:T(8,128)S(1)} %all_gather.15), kind=kOutput, calls=%fused_computation.30 | convolution fusion | flops 805306368 | bytes 2883584 | tf_op jit(solution)/shard_map/dot_general | solution.py:35
  121.8 0.0 reduce-scatter.5.cloned.1.call-update
  121.9 31.9 %reduce-scatter.5.cloned.1.call-done = f32[128,128]{1,0:T(8,128)} async-done(((f32[1024,128]{1,0:T(8,128)}), f32[128,128]{1,0:T(8,128)}) %reduce-scatter.5.cloned.1.call-update) | async-done | bytes 65552 | tf_op jit(solution)/shard_map/reduce_scatter | solution.py:34
  153.8 0.0 copy-done
  153.8 1.0 fusion.13
  154.7 12.1 %all-reduce = (f32[128]{0:T(128)S(1)}, f32[128]{0:T(128)S(1)}) all-reduce(f32[128]{0:T(128)S(1)} %get-tuple-element.6, f32[128]{0:T(128)S(1)} %get-tuple-element.5), channel_id=1, replica_groups=mesh['row'=4,'col'=8] {'col'}, use_global_device_ids=true, to_apply=%region_16.0 | all-reduce | flops 256 | bytes 2048 | tf_op jit(solution)/shard_map/psum | solution.py:41
  166.9 11.7 %all-reduce.2 = (f32[128]{0:T(128)S(1)}, f32[128]{0:T(128)S(1)}) all-reduce(f32[128]{0:T(128)S(1)} %get-tuple-element.9, f32[128]{0:T(128)S(1)} %get-tuple-element.10), channel_id=1, replica_groups=mesh['row'=4,'col'=8] {'row'}, use_global_device_ids=true, to_apply=%region_17.0 | all-reduce | flops 256 | bytes 2048 | tf_op jit(solution)/shard_map/psum | solution.py:40
  178.5 1.0 fusion.12
  179.5 1.0 exponential_reduce_fusion
  180.5 1.6 subtract_subtract_fusion
  (5 shorter events, 0.0 us)
Async XLA Ops:
  6.5 28.8 %all-gather.3.cloned.1.call-start = ((), (), s32[]{:S(2)}) async-start(), calls=%async_computation.2 | async-start | bytes 1179648 | tf_op jit(solution)/shard_map/all_gather | solution.py:13
  7.3 70.4 %reduce-scatter.3.cloned.1.call-start = ((), (), s32[]{:S(2)}) async-start(), calls=%async_computation.3 | async-start | bytes 589824 | tf_op jit(solution)/shard_map/reduce_scatter | solution.py:34
  40.7 37.0 %copy-start.1 = (s32[128]{0:T(128)S(1)}, s32[128]{0:T(128)}, u32[]{:S(2)}) copy-start(s32[128]{0:T(128)} %param.3) | copy-start | bytes 1540
  43.4 110.4 %reduce-scatter.5.cloned.1.call-start = ((), (), s32[]{:S(2)}) async-start(), calls=%async_computation.4 | async-start | bytes 589824 | tf_op jit(solution)/shard_map/reduce_scatter | solution.py:34
  77.6 76.1 %copy-start = (f32[128,128]{1,0:T(8,128)S(1)}, f32[128,128]{1,0:T(8,128)}, u32[]{:S(2)}) copy-start(f32[128,128]{1,0:T(8,128)} %reduce-scatter.3.cloned.1.call-done) | copy-start | bytes 196612
Sparse Core Ops, SparseCore 0:
  9.2 26.0 all-gather.2
  43.5 34.1 reduce-scatter.2
  122.0 31.7 reduce-scatter.4
